TPU v7x, 512 devices: a whole 4x8x8 slice. The times are simulated.
512 devices in a mesh: section: 4 (over z_lo, core), cls: 128 (over z_hi, x, y).
Axes of the slice: x: 4, y: 8, z: 8 (z_hi: 4, z_lo: 2; z = z_hi * 2 + z_lo), core: 2. Of those that a mesh axis runs over, the one named last changes fastest.
Arguments:
- images: bfloat16 [8192, 256, 256], P(('section', 'cls')), may hold values from -6 to 6
- group_ids: int32 [8192], P(('section', 'cls')), may hold values from 0 to 3
- row_filters: bfloat16 [4, 256, 256], replicated, may hold values from -0.375 to 0.375
- column_filters: bfloat16 [4, 256, 256], replicated, may hold values from -0.375 to 0.375
- basis_rows: bfloat16 [256, 16], replicated, may hold values from -0.375 to 0.375
- basis_columns: bfloat16 [256, 16], replicated, may hold values from -0.375 to 0.375
- rotations: bfloat16 [36, 256, 256], P('section'), may hold values from -0.375 to 0.375
- references: bfloat16 [256, 256], P('cls'), may hold values from -2 to 2
- sharpness: bfloat16 [8192], P(('section', 'cls')), may hold values from 0.049804688 to 2
- best_rotation: int32 [8192], P(('section', 'cls')), may hold values from 0 to 35
- assignments: int32 [8192, 32], P(('section', 'cls')), may hold values from 0 to 255, all different within a row; in each aligned block of 16 rows (0 to 15, 16 to 31, ...) at most 2 rows name the same one
Outputs:
- new_references: float32 [256, 256], P('cls')
- evidence: float32 [8192], P(('section', 'cls'))
Inputs may be any that keep to these rules, and one draw needn't show every extreme that they name: `assignments`: each particle lists 32 different classes; among the particles of one device no class is listed more than 2 times, a bound that some block reaches.
All inputs are finite; a program needn't handle non-finite values.
Results may differ from a plain program's by a relative error of at most 0.019.
Values may be sent and summed in bfloat16 or wider, within the bound.
A program may use at most 64 MiB of HBM per device.

v0:
```python
import math

import jax
import jax.numpy as jnp
from jax import lax
from jax.sharding import PartitionSpec as P

EPSILON = 1e-05


def soft_edge(pixels):
    coordinate = (jnp.arange(pixels, dtype=jnp.float32) - (pixels - 1) / 2.0) / (pixels / 2.0)
    radius = jnp.sqrt(
        coordinate[:, None] * coordinate[:, None] + coordinate[None, :] * coordinate[None, :]
    )
    falloff = jnp.clip((radius - 0.8) / 0.15, 0.0, 1.0)
    return 0.5 + 0.5 * jnp.cos(math.pi * falloff)


def filter_images(images, group_ids, row_filters, column_filters, basis_rows, basis_columns):
    column_each = jnp.take(column_filters, group_ids, axis=0)
    row_each = jnp.take(row_filters, group_ids, axis=0)
    filtered_half = jnp.einsum(
        "bij,bjk->bik", images, column_each, preferred_element_type=jnp.float32
    ).astype(jnp.bfloat16)
    filtered = jnp.einsum(
        "bij,bjk->bik", row_each, filtered_half, preferred_element_type=jnp.float32
    )
    masked = filtered * soft_edge(images.shape[1])
    power = jnp.mean(masked * masked, axis=(1, 2), keepdims=True)
    normed = (masked * lax.rsqrt(power + EPSILON)).astype(jnp.bfloat16)
    inner = jnp.einsum("bij,jk->bik", normed, basis_columns, preferred_element_type=jnp.float32)
    coeffs = jnp.einsum(
        "ja,bjk->bak", basis_rows.astype(jnp.float32), inner, precision=lax.Precision.HIGHEST
    )
    return coeffs.reshape(coeffs.shape[0], -1).astype(jnp.bfloat16)


def body(
    images,
    group_ids,
    row_filters,
    column_filters,
    basis_rows,
    basis_columns,
    rotations,
    references,
    sharpness,
    best_rotation,
    assignments,
):
    particles = images.shape[0]
    listed = assignments.shape[1]
    coeffs = filter_images(
        images, group_ids, row_filters, column_filters, basis_rows, basis_columns
    )
    gathered, gathered_sharp = (
        lax.all_gather(coeffs, "section", axis=0, tiled=True),
        lax.all_gather(sharpness, "section", axis=0, tiled=True),
    )
    gathered_best = lax.all_gather(best_rotation, "section", axis=0, tiled=True)
    all_refs = lax.all_gather(references, "cls", axis=0, tiled=True)
    classes = all_refs.shape[0]
    width = all_refs.shape[1]
    sections = lax.axis_size("section")
    local_rotations = rotations.shape[0]
    first_rotation = lax.axis_index("section") * local_rotations
    turned = jnp.einsum(
        "rkl,nl->nrk", rotations, gathered, preferred_element_type=jnp.float32
    ).astype(jnp.bfloat16)
    products = jnp.einsum("nrk,ck->nrc", turned, all_refs, preferred_element_type=jnp.float32)
    scores = products * gathered_sharp.astype(jnp.float32)[:, None, None]
    maxima = jnp.max(scores, axis=1)
    totals = jnp.sum(jnp.exp(scores - maxima[:, None, :]), axis=1)
    partial_marg = (maxima + jnp.log(totals)).reshape(sections, particles, classes)
    received_marg = lax.all_to_all(partial_marg, "section", split_axis=0, concat_axis=0, tiled=True)
    own_marg = jax.nn.logsumexp(received_marg, axis=0)
    evidence = jax.nn.logsumexp(own_marg, axis=1)
    class_range = jnp.arange(classes, dtype=jnp.int32)
    matches = assignments[:, :, None] == class_range[None, None, :]
    picked = jnp.sum(jnp.where(matches, own_marg[:, None, :], 0.0), axis=2)
    weights = jax.nn.softmax(picked, axis=1).astype(jnp.bfloat16)
    offset = gathered_best - first_rotation
    chosen = (offset[:, None] == jnp.arange(local_rotations, dtype=jnp.int32)[None, :]).astype(
        jnp.bfloat16
    )
    partial_rows = jnp.einsum("nrk,nr->nk", turned, chosen, preferred_element_type=jnp.float32)
    aligned = lax.psum_scatter(
        partial_rows.astype(jnp.bfloat16), "section", scatter_dimension=0, tiled=True
    )
    contribution = (
        weights.astype(jnp.float32)[:, :, None] * aligned.astype(jnp.float32)[:, None, :]
    ).astype(jnp.bfloat16)
    flat_classes = assignments.reshape(-1)
    flat_contribution = contribution.reshape(-1, width)
    flat_weights = weights.reshape(-1)
    owners = lax.axis_size("cls")
    own_classes = references.shape[0]
    capacity = max(2, -(-(particles * listed) // classes))
    onehot = (flat_classes[:, None] == class_range[None, :]).astype(jnp.int32)
    slot_rank = jnp.sum((jnp.cumsum(onehot, axis=0) - 1) * onehot, axis=1)
    slot_index = flat_classes * capacity + slot_rank
    buffer = (
        jnp.zeros((classes * capacity, width), jnp.bfloat16).at[slot_index].set(flat_contribution)
    )
    weight_slots = jnp.zeros((classes * capacity,), jnp.bfloat16).at[slot_index].set(flat_weights)
    buffer = buffer.reshape(owners, own_classes, capacity, width)
    weight_slots = weight_slots.reshape(owners, own_classes, capacity)
    received, received_weights = (
        lax.all_to_all(buffer, "cls", split_axis=0, concat_axis=0, tiled=True),
        lax.all_to_all(weight_slots, "cls", split_axis=0, concat_axis=0, tiled=True),
    )
    class_sums = jnp.sum(received.astype(jnp.float32), axis=(0, 2))
    class_weights = jnp.sum(received_weights.astype(jnp.float32), axis=(0, 2))
    class_sums, class_weights = lax.psum((class_sums, class_weights), "section")
    new_references = (class_sums + references.astype(jnp.float32)) / (class_weights[:, None] + 1.0)
    return (new_references, evidence)


def solution(mesh):
    in_specs = (
        P(("section", "cls"), None, None),
        P(("section", "cls")),
        P(),
        P(),
        P(),
        P(),
        P("section", None, None),
        P("cls", None),
        P(("section", "cls")),
        P(("section", "cls")),
        P(("section", "cls"), None),
    )
    out_specs = (P("cls", None), P(("section", "cls")))
    return jax.shard_map(body, mesh=mesh, in_specs=in_specs, out_specs=out_specs, check_vma=False)
```

profile of v0, /device:TPU:1, one launch (start us, length us, event | category | flops | bytes accessed | tf_op | source)
XLA Modules:
  0.0 496.1 jit_solution(2594808979812159641)
XLA Ops:
  7.2 0.8 compare_select_fusion.1
  8.0 0.7 compare_and_fusion
  8.7 3.1 gather_fusion
  11.8 2.0 gather_fusion.1
  13.8 1.0 multiply_add_fusion
  14.9 5.7 %multiply_reduce_fusion = (f32[16]{0:T(128)S(1)}, f32[16,256,256]{2,1,0:T(8,128)}) fusion(f32[256,256]{1,0:T(8,128)S(1)} %multiply_add_fusion, bf16[16,256,256]{2,1,0:T(8,128)(2,1)S(1)} %copy-done, bf16[16,256,256]{2,1,0:T(8,128)(2,1)} %gather_fusion.1, pred[16]{0:T(512)(128)(4,1)S(1)} %compare_and_fusion, bf16[16,256,256]{2,1,0:T(8,128)(2,1)} %gather_fusion), kind=kOutput, calls=%fused_computation.5 | convolution fusion | flops 1080033280 | bytes 10747984 | tf_op jit(solution)/shard_map/bij,bjk->bik/dot_general | solution.py:26
  20.6 3.0 fusion
  23.6 0.3 fusion.14
  24.1 12.3 %all_gather.12 = bf16[64,256]{1,0:T(8,128)(2,1)} all-gather(bf16[16,256]{1,0:T(8,128)(2,1)S(1)} %convert_element_type.71), channel_id=1, replica_groups=mesh['section'=4,'cls'=128] {'section'}, dimensions={0}, use_global_device_ids=true | all-gather | bytes 40960 | tf_op jit(solution)/shard_map/all_gather | solution.py:58
  36.4 1.3 dynamic-slice
  38.6 5.2 %all-reduce = bf16[64]{0:T(256)(128)(2,1)S(1)} all-reduce(bf16[64]{0:T(256)(128)(2,1)S(1)} %dynamic-update-slice), channel_id=1, replica_groups=mesh['section'=4,'cls'=128] {'section'}, use_global_device_ids=true, to_apply=%add | all-reduce | flops 64 | bytes 256
  43.8 320.0 %all-gather = bf16[128,2,256]{2,1,0:T(2,128)(2,1)S(1)} all-gather(bf16[1,2,256]{2,1,0:T(2,128)(2,1)S(1)} %bitcast.40), channel_id=1, replica_groups=mesh['section'=4,'cls'=128] {'cls'}, dimensions={0}, use_global_device_ids=true | all-gather | bytes 132096 | tf_op jit(solution)/shard_map/all_gather | solution.py:62
  363.9 1.3 convolution_convert_fusion
  365.1 0.3 fusion.39
  365.5 0.3 copy-done.3
  365.8 0.6 log_add_fusion
  366.5 60.8 %all-to-all-start = ((f32[4,16,256]{2,1,0:T(8,128)}), f32[4,16,256]{2,1,0:T(8,128)S(1)}, u32[]{:S(2)}, u32[]{:S(2)}) async-start(f32[4,16,256]{2,1,0:T(8,128)} %bitcast.11), calls=%async_computation | async-start | bytes 131072 | tf_op jit(solution)/shard_map/all_to_all | solution.py:76
  427.6 4.2 all-reduce.1
  431.9 1.3 fusion.19
  433.2 0.6 copy.50
  435.8 3.8 scatter_custom_fusion.1
  439.6 0.8 reshape.197
  440.4 6.3 %all-to-all-start.2 = ((bf16[128,2,2]{2,1,0:T(2,128)(2,1)}), bf16[128,2,2]{2,1,0:T(2,128)(2,1)S(1)}, u32[]{:S(2)}, u32[]{:S(2)}) async-start(bf16[128,2,2]{2,1,0:T(2,128)(2,1)} %reshape.197), calls=%async_computation.3 | async-start | bytes 131072 | tf_op jit(solution)/shard_map/all_to_all | solution.py:111
  446.8 0.7 convert_element_type.78
  447.6 2.4 scatter_custom_fusion
  450.0 0.8 reshape.196
  450.8 8.5 %all-to-all-done.2 = bf16[128,2,2]{2,1,0:T(2,128)(2,1)S(1)} async-done(((bf16[128,2,2]{2,1,0:T(2,128)(2,1)}), bf16[128,2,2]{2,1,0:T(2,128)(2,1)S(1)}, u32[]{:S(2)}, u32[]{:S(2)}) %all-to-all-start.2) | async-done | bytes 1056 | tf_op jit(solution)/shard_map/all_to_all | solution.py:111
  459.3 7.2 %all-to-all-start.1 = ((bf16[128,2,2,256]{3,2,1,0:T(2,128)(2,1)}), bf16[128,2,2,256]{3,2,1,0:T(2,128)(2,1)S(1)}, u32[]{:S(2)}, u32[]{:S(2)}) async-start(bf16[128,2,2,256]{3,2,1,0:T(2,128)(2,1)} %reshape.196), calls=%async_computation.2 | async-start | bytes 524288 | tf_op jit(solution)/shard_map/all_to_all | solution.py:110
  466.7 0.5 log_add_fusion.2
  467.5 12.7 %all-to-all-done.1 = bf16[128,2,2,256]{3,2,1,0:T(2,128)(2,1)S(1)} async-done(((bf16[128,2,2,256]{3,2,1,0:T(2,128)(2,1)}), bf16[128,2,2,256]{3,2,1,0:T(2,128)(2,1)S(1)}, u32[]{:S(2)}, u32[]{:S(2)}) %all-to-all-start.1) | async-done | bytes 262176 | tf_op jit(solution)/shard_map/all_to_all | solution.py:110
  480.3 8.3 %all-reduce.2 = (f32[2,256]{1,0:T(2,128)S(1)}, f32[2]{0:T(128)S(1)}) all-reduce(f32[2,256]{1,0:T(2,128)S(1)} %convert_reduce_fusion, f32[2]{0:T(128)S(1)} %convert_reduce_fusion.1), channel_id=1, replica_groups=mesh['section'=4,'cls'=128] {'section'}, use_global_device_ids=true, to_apply=%region_14.16 | all-reduce | flops 514 | bytes 4112 | tf_op jit(solution)/shard_map/psum | solution.py:115
  488.6 0.7 add_divide_fusion
  (66 shorter events, 3.7 us)
Async XLA Ops:
  7.2 7.7 %copy-start = (bf16[16,256,256]{2,1,0:T(8,128)(2,1)S(1)}, bf16[16,256,256]{2,1,0:T(8,128)(2,1)}, u32[]{:S(2)}) copy-start(bf16[16,256,256]{2,1,0:T(8,128)(2,1)} %param.13) | copy-start | bytes 6291460
  8.7 3.1 copy-start.1
  14.9 5.7 %copy-start.5 = (bf16[256,16]{0,1:T(8,128)(2,1)S(1)}, bf16[256,16]{0,1:T(8,128)(2,1)}, u32[]{:S(2)}) copy-start(bf16[256,16]{0,1:T(8,128)(2,1)} %param.18) | copy-start | bytes 24580
  20.6 3.1 copy-start.6
  20.6 17.8 %copy-start.8 = (bf16[16]{0:T(256)(128)(2,1)S(1)}, bf16[16]{0:T(256)(128)(2,1)}, u32[]{:S(2)}) copy-start(bf16[16]{0:T(256)(128)(2,1)} %param.21) | copy-start | bytes 100
  20.6 23.2 %copy-start.7 = (bf16[2,256]{1,0:T(2,128)(2,1)S(1)}, bf16[2,256]{1,0:T(2,128)(2,1)}, u32[]{:S(2)}) copy-start(bf16[2,256]{1,0:T(2,128)(2,1)} %param.20) | copy-start | bytes 3076
  20.6 343.3 %copy-start.2 = (bf16[9,256,256]{2,1,0:T(8,128)(2,1)S(1)}, bf16[9,256,256]{2,1,0:T(8,128)(2,1)}, u32[]{:S(2)}) copy-start(bf16[9,256,256]{2,1,0:T(8,128)(2,1)} %param.19) | copy-start | bytes 3538948
  24.0 403.3 %copy-start.9 = (s32[16]{0:T(128)S(1)}, s32[16]{0:T(128)}, u32[]{:S(2)}) copy-start(s32[16]{0:T(128)} %param.22) | copy-start | bytes 196
  363.8 70.0 %copy-start.4 = (s32[16,32]{1,0:T(8,128)S(1)}, s32[16,32]{1,0:T(8,128)}, u32[]{:S(2)}) copy-start(s32[16,32]{1,0:T(8,128)} %param.23) | copy-start | bytes 6148
  365.1 0.7 copy-start.3
  366.5 68.4 %all-to-all-start = ((f32[4,16,256]{2,1,0:T(8,128)}), f32[4,16,256]{2,1,0:T(8,128)S(1)}, u32[]{:S(2)}, u32[]{:S(2)}) async-start(f32[4,16,256]{2,1,0:T(8,128)} %bitcast.11), calls=%async_computation | async-start | bytes 131072 | tf_op jit(solution)/shard_map/all_to_all | solution.py:76
  427.3 19.4 %reduce-scatter.2.cloned.1.call-start = ((), (), s32[]{:S(2)}) async-start(), calls=%async_computation.4 | async-start | bytes 40960 | tf_op jit(solution)/shard_map/reduce_scatter | solution.py:88
  440.4 18.9 %all-to-all-start.2 = ((bf16[128,2,2]{2,1,0:T(2,128)(2,1)}), bf16[128,2,2]{2,1,0:T(2,128)(2,1)S(1)}, u32[]{:S(2)}, u32[]{:S(2)}) async-start(bf16[128,2,2]{2,1,0:T(2,128)(2,1)} %reshape.197), calls=%async_computation.3 | async-start | bytes 131072 | tf_op jit(solution)/shard_map/all_to_all | solution.py:111
  459.3 20.9 %all-to-all-start.1 = ((bf16[128,2,2,256]{3,2,1,0:T(2,128)(2,1)}), bf16[128,2,2,256]{3,2,1,0:T(2,128)(2,1)S(1)}, u32[]{:S(2)}, u32[]{:S(2)}) async-start(bf16[128,2,2,256]{3,2,1,0:T(2,128)(2,1)} %reshape.196), calls=%async_computation.2 | async-start | bytes 524288 | tf_op jit(solution)/shard_map/all_to_all | solution.py:110
Sparse Core Ops, SparseCore 0:
  433.9 11.9 reduce-scatter.1
where the time goes:
time: 497 us; the launch traced here: 496 us
  blocking collectives  350 us (70%)
  starting transfers between devices  74.3 us (15%)
  waiting for transfers between devices  21.3 us (4%)
  local copies, waits for them, and re-layouts  16.5 us (3%)
  between operations  15 us (3%)
  matrix products  11.8 us (2%)
  other arithmetic  7.26 us (1%)
    all_gather x1, blocking collectives, body(): all_refs = lax.all_gather(references, 'cls', axis=0, tiled=True)  320 us
    all_to_all x1, starting transfers between devices, body(): lax.all_to_all(partial_marg, 'section', split_axis=0, concat_axis=0, tile...  60.8 us
    all_to_all x1, waiting for transfers between devices, body(): lax.all_to_all(buffer, 'cls', split_axis=0, concat_axis=0, tiled=True)  12.7 us
    all_gather x1, blocking collectives, body(): lax.all_gather(coeffs, 'section', axis=0, tiled=True)  12.3 us
  transfers between devices with their start and end apart: 4, of which 2 were waited for; matrix products, arithmetic and copies ran while one was open for 3% of the time, Pallas kernels for 0%

commit v1 on v0

v1 whole, which is shorter than its diff:
```python
import functools
import math

import jax
import jax.numpy as jnp
import numpy as np
from jax import lax
from jax.experimental import pallas as pl
from jax.experimental.pallas import tpu as pltpu
from jax.sharding import PartitionSpec as P

EPSILON = 1e-05
TORUS = (4, 4, 8)
MESH = pl.DeviceIdType.MESH
LANES = 128


def soft_edge(pixels):
    coordinate = (np.arange(pixels, dtype=np.float32) - np.float32((pixels - 1) / 2.0)) / np.float32(pixels / 2.0)
    radius = np.sqrt(coordinate[:, None] * coordinate[:, None] + coordinate[None, :] * coordinate[None, :])
    falloff = np.clip((radius - np.float32(0.8)) / np.float32(0.15), 0.0, 1.0)
    return (0.5 + 0.5 * np.cos(math.pi * falloff)).astype(np.float32)


def contract_last(a, b):
    return lax.dot_general(a, b, (((1,), (1,)), ((), ())), preferred_element_type=jnp.float32)


def contract_first(a, b):
    return lax.dot_general(a, b, (((0,), (0,)), ((), ())), preferred_element_type=jnp.float32)


def kernel(
    dims,
    images,
    group_ids,
    row_filters,
    column_filters,
    basis_rows,
    basis_columns,
    mask,
    rotations,
    references,
    sharpness,
    best_rotation,
    assignments,
    new_references,
    evidence,
    img,
    rowf,
    colf,
    edge,
    rot,
    bas,
    tiled,
    spread,
    raw,
    squares,
    near,
    refs,
    coef,
    turned_out,
    turned_in,
    marg_out,
    marg_in,
    sum_x,
    got_x,
    sum_y,
    got_y,
    sum_z,
    got_z,
    img_sem,
    in_sem,
    send_sem,
    recv_sem,
):
    nz, nx, ny = dims
    section, cls = lax.axis_index("section"), lax.axis_index("cls")
    sections = 4
    zh = cls // (nx * ny)
    xx = (cls // ny) % nx
    yy = cls % ny
    particles, pix = img.shape[0], img.shape[1]
    local = rot.shape[0]
    width = rot.shape[1]
    classes = nz * nx * ny * 2
    nb = bas.shape[1]

    def at(dz, dx, dy, ds):
        return {
            "section": (section + ds) % sections,
            "cls": (((zh + dz) % nz) * nx + (xx + dx) % nx) * ny + (yy + dy) % ny,
        }

    peers = [at(0, dx, 0, 0) for dx in range(1, nx)]
    peers += [at(0, 0, dy, 0) for dy in range(1, ny)]
    peers += [at(dz, 0, 0, ds) for dz in range(nz) for ds in range(sections) if (dz, ds) != (0, 0)]
    barrier = pltpu.get_barrier_semaphore()
    for peer in peers:
        pl.semaphore_signal(barrier, inc=1, device_id=peer, device_id_type=MESH)

    inputs = {}
    for k, (src, dst) in enumerate(
        [
            (column_filters, colf),
            (row_filters, rowf),
            (basis_rows, bas.at[0]),
            (basis_columns, bas.at[1]),
            (mask, edge),
            (rotations, rot),
        ]
    ):
        inputs[k] = pltpu.make_async_copy(src, dst, in_sem.at[k])
    for k in (2, 3, 0):
        inputs[k].start()
    pltpu.make_async_copy(images.at[0], img.at[0], img_sem.at[0]).start()
    for k in (1, 4):
        inputs[k].start()

    @pl.loop(1, particles)
    def _(n):
        pltpu.make_async_copy(images.at[n], img.at[n], img_sem.at[n]).start()

    inputs[5].start()

    inputs[2].wait()
    inputs[3].wait()
    row_at = lax.broadcasted_iota(jnp.int32, (nb, nb * nb), 0)
    lane_at = lax.broadcasted_iota(jnp.int32, (nb, nb * nb), 1)
    minor = (lane_at % nb == row_at).astype(jnp.float32).astype(jnp.bfloat16)
    major = (lane_at // nb == row_at).astype(jnp.float32).astype(jnp.bfloat16)
    tiled[...] = contract_first(bas[1], minor).astype(jnp.bfloat16)
    spread[...] = contract_first(bas[0], major)
    inputs[0].wait()
    inputs[1].wait()
    inputs[4].wait()

    def filter_image(n):
        pltpu.make_async_copy(images.at[n], img.at[n], img_sem.at[n]).wait()
        group = group_ids[n]
        half = jnp.dot(img[n], colf[group], preferred_element_type=jnp.float32).astype(jnp.bfloat16)
        masked = jnp.dot(rowf[group], half, preferred_element_type=jnp.float32) * edge[...]
        inner = jnp.dot(masked.astype(jnp.bfloat16), tiled[...], preferred_element_type=jnp.float32)
        squares[pl.ds(n, 1), :] = jnp.sum(masked * masked, axis=0, keepdims=True)
        raw[pl.ds(n, 1), :] = jnp.sum(inner * spread[...], axis=0, keepdims=True)

    def filter_images(low, high, together):
        @pl.loop(low, high, step=together)
        def _(n):
            for k in range(together):
                filter_image(n + k)

    def send(k, src, dst, to):
        pltpu.make_async_remote_copy(
            src_ref=src,
            dst_ref=dst,
            send_sem=send_sem.at[k],
            recv_sem=recv_sem.at[k],
            device_id=to,
            device_id_type=MESH,
        ).start()

    def arrived(k, ref):
        pltpu.make_async_copy(ref, ref, recv_sem.at[k]).wait()

    def sent(k, ref):
        pltpu.make_async_copy(ref, ref, send_sem.at[k]).wait()

    quarter = particles // 4
    filter_images(0, quarter, 2)

    pl.semaphore_wait(barrier, len(peers))
    near[0] = references[...].astype(jnp.float32).astype(jnp.bfloat16)
    for dz in range(1, nz):
        send(0, near.at[0], near.at[nz - dz], at(dz, 0, 0, 0))
    filter_images(quarter, 2 * quarter, 2)
    arrived(0, near.at[pl.ds(1, nz - 1)])
    refs[0, 0] = jnp.concatenate([near[dz].astype(jnp.float32) for dz in range(nz)], axis=0).astype(jnp.bfloat16)
    for dy in range(1, ny):
        send(1, refs.at[0, 0], refs.at[0, ny - dy], at(0, 0, dy, 0))
    filter_images(2 * quarter, 3 * quarter, 2)
    arrived(1, refs.at[0, pl.ds(1, ny - 1)])
    for dx in range(1, nx):
        send(2, refs.at[0], refs.at[nx - dx], at(0, dx, 0, 0))
    filter_images(3 * quarter, particles, 2)

    eye = lax.broadcasted_iota(jnp.int32, (particles, particles), 0) == lax.broadcasted_iota(
        jnp.int32, (particles, particles), 1
    )
    sharp_row = sharpness[...].astype(jnp.float32)
    sharp = jnp.sum(jnp.where(eye, jnp.broadcast_to(sharp_row, (particles, particles)), 0.0), axis=1, keepdims=True)
    best_row = best_rotation[...].astype(jnp.float32)
    best = jnp.sum(jnp.where(eye, jnp.broadcast_to(best_row, (particles, particles)), 0.0), axis=1, keepdims=True)
    power = jnp.sum(squares[...], axis=1, keepdims=True) * (1.0 / (pix * pix))
    scale = lax.rsqrt(power + EPSILON) * sharp
    coef[0, :, 0:width] = (raw[...] * scale).astype(jnp.bfloat16)
    coef[0, :, width:] = jnp.broadcast_to(best, (particles, LANES)).astype(jnp.bfloat16)
    for ds in range(1, sections):
        send(3, coef.at[0], coef.at[sections - ds], at(0, 0, 0, ds))

    place = lax.broadcasted_iota(jnp.int32, (particles, classes), 1)
    dx_at, rest = place // (ny * nz * 2), place % (ny * nz * 2)
    dy_at, rest = rest // (nz * 2), rest % (nz * 2)
    dz_at, last = rest // 2, rest % 2
    name = ((((zh + dz_at) % nz) * nx + (xx + dx_at) % nx) * ny + (yy + dy_at) % ny) * 2 + last
    listed = jnp.zeros((particles, classes), jnp.float32)
    for j in range(assignments.shape[1]):
        listed = jnp.where(assignments[:, j : j + 1] == name, 1.0, listed)

    inputs[5].wait()
    arrived(2, refs.at[pl.ds(1, nx - 1)])
    all_refs = refs[...].astype(jnp.float32).reshape(classes, width).astype(jnp.bfloat16)
    arrived(3, coef.at[pl.ds(1, sections - 1)])

    everyone = sections * particles
    gathered = coef[:, :, 0:width].reshape(everyone, width)
    best_all = coef[:, :, width:].astype(jnp.float32).reshape(everyone, LANES)
    best_all = jnp.concatenate([best_all] * (width // LANES), axis=1)
    first = (section * local).astype(jnp.float32)
    aligned = jnp.zeros((everyone, width), jnp.float32)
    turned = []
    for r in range(local):
        one = contract_last(gathered, rot[r])
        aligned = jnp.where(best_all == first + float(r), one, aligned)
        turned.append(one.astype(jnp.bfloat16))
    turned_out[...] = aligned.astype(jnp.bfloat16).reshape(sections, particles, width)
    for ds in range(1, sections):
        send(4, turned_out.at[ds], turned_in.at[sections - ds], at(0, 0, 0, ds))
    scores = [contract_last(one, all_refs) for one in turned]
    largest = functools.reduce(jnp.maximum, scores)
    total = functools.reduce(jnp.add, [jnp.exp(one - largest) for one in scores])
    marg_out[...] = (largest + jnp.log(total)).reshape(sections, particles, classes)
    for ds in range(1, sections):
        send(5, marg_out.at[ds], marg_in.at[sections - ds], at(0, 0, 0, ds))

    arrived(4, turned_in.at[pl.ds(1, sections - 1)])
    mine = functools.reduce(
        jnp.add, [turned_out[0].astype(jnp.float32)] + [turned_in[d].astype(jnp.float32) for d in range(1, sections)]
    )
    mine = (mine * (1.0 / sharp)).astype(jnp.bfloat16)
    with_one = jnp.concatenate([mine, jnp.ones((particles, LANES), jnp.bfloat16)], axis=1)
    arrived(5, marg_in.at[pl.ds(1, sections - 1)])
    parts = [marg_out[0]] + [marg_in[d] for d in range(1, sections)]
    largest = functools.reduce(jnp.maximum, parts)
    marg = largest + jnp.log(functools.reduce(jnp.add, [jnp.exp(one - largest) for one in parts]))
    highest = jnp.max(jnp.where(listed > 0.0, marg, -jnp.inf), axis=1, keepdims=True)
    weight = jnp.where(listed > 0.0, jnp.exp(marg - highest), 0.0)
    weight = (weight / jnp.sum(weight, axis=1, keepdims=True)).astype(jnp.bfloat16)
    sums = contract_first(weight, with_one)
    sum_x[...] = sums.astype(jnp.bfloat16).reshape(sum_x.shape)
    for dx in range(1, nx):
        send(6, sum_x.at[dx], got_x.at[dx], at(0, dx, 0, 0))

    peak = jnp.max(marg, axis=1, keepdims=True)
    proof = peak + jnp.log(jnp.sum(jnp.exp(marg - peak), axis=1, keepdims=True))
    evidence[...] = jnp.sum(jnp.where(eye, jnp.broadcast_to(proof, (particles, particles)), 0.0), axis=0, keepdims=True)

    arrived(6, got_x.at[pl.ds(1, nx - 1)])
    total = functools.reduce(
        jnp.add, [sum_x[0].astype(jnp.float32)] + [got_x[d].astype(jnp.float32) for d in range(1, nx)]
    )
    sum_y[...] = total.reshape(sum_y.shape).astype(jnp.bfloat16)
    for dy in range(1, ny):
        send(7, sum_y.at[dy], got_y.at[dy], at(0, 0, dy, 0))
    arrived(7, got_y.at[pl.ds(1, ny - 1)])
    total = functools.reduce(
        jnp.add, [sum_y[0].astype(jnp.float32)] + [got_y[d].astype(jnp.float32) for d in range(1, ny)]
    )
    for dz in range(nz):
        sum_z[dz] = total[2 * dz : 2 * dz + 2]
    for dz in range(nz):
        for ds in range(sections):
            if (dz, ds) != (0, 0):
                send(8, sum_z.at[dz], got_z.at[dz * sections + section], at(dz, 0, 0, ds))
    got_z[section] = sum_z[0]
    arrived(8, got_z.at[pl.ds(0, nz * sections - 1)])
    total = functools.reduce(jnp.add, [got_z[d] for d in range(nz * sections)])
    over = total[:, width:] + 1.0
    over = jnp.concatenate([over] * (width // LANES), axis=1)
    new_references[...] = (total[:, 0:width] + references[...].astype(jnp.float32)) / over

    sent(0, near.at[pl.ds(1, nz - 1)])
    sent(1, refs.at[0, pl.ds(1, ny - 1)])
    sent(2, refs.at[pl.ds(1, nx - 1)])
    sent(3, coef.at[pl.ds(1, sections - 1)])
    sent(4, turned_out.at[pl.ds(1, sections - 1)])
    sent(5, marg_out.at[pl.ds(1, sections - 1)])
    sent(6, sum_x.at[pl.ds(1, nx - 1)])
    sent(7, sum_y.at[pl.ds(1, ny - 1)])
    sent(8, got_z.at[pl.ds(0, nz * sections - 1)])


def body(
    dims,
    images,
    group_ids,
    row_filters,
    column_filters,
    basis_rows,
    basis_columns,
    rotations,
    references,
    sharpness,
    best_rotation,
    assignments,
):
    nz, nx, ny = dims
    sections = 4
    particles, pix = images.shape[0], images.shape[1]
    nb = basis_rows.shape[1]
    local, width = rotations.shape[0], rotations.shape[1]
    classes = 2 * nz * nx * ny
    wide = width + LANES
    bf16, f32 = jnp.bfloat16, jnp.float32
    hbm = pl.BlockSpec(memory_space=pltpu.HBM)
    vmem = pl.BlockSpec(memory_space=pltpu.VMEM)
    smem = pl.BlockSpec(memory_space=pltpu.SMEM)
    new_references, evidence = pl.pallas_call(
        functools.partial(kernel, dims),
        out_shape=(
            jax.ShapeDtypeStruct((2, width), f32),
            jax.ShapeDtypeStruct((1, particles), f32),
        ),
        in_specs=[hbm, smem, hbm, hbm, hbm, hbm, hbm, hbm, vmem, vmem, vmem, vmem],
        out_specs=(vmem, vmem),
        scratch_shapes=[
            pltpu.VMEM((particles, pix, pix), bf16),
            pltpu.VMEM(row_filters.shape, bf16),
            pltpu.VMEM(column_filters.shape, bf16),
            pltpu.VMEM((pix, pix), f32),
            pltpu.VMEM(rotations.shape, bf16),
            pltpu.VMEM((2, nb, pix), bf16),
            pltpu.VMEM((pix, nb * nb), bf16),
            pltpu.VMEM((pix, nb * nb), f32),
            pltpu.VMEM((particles, nb * nb), f32),
            pltpu.VMEM((particles, pix), f32),
            pltpu.VMEM((nz, 2, width), bf16),
            pltpu.VMEM((nx, ny, 2 * nz, width), bf16),
            pltpu.VMEM((sections, particles, wide), bf16),
            pltpu.VMEM((sections, particles, width), bf16),
            pltpu.VMEM((sections, particles, width), bf16),
            pltpu.VMEM((sections, particles, classes), f32),
            pltpu.VMEM((sections, particles, classes), f32),
            pltpu.VMEM((nx, 2 * ny * nz, wide), bf16),
            pltpu.VMEM((nx, 2 * ny * nz, wide), bf16),
            pltpu.VMEM((ny, 2 * nz, wide), bf16),
            pltpu.VMEM((ny, 2 * nz, wide), bf16),
            pltpu.VMEM((nz, 2, wide), f32),
            pltpu.VMEM((nz * sections, 2, wide), f32),
            pltpu.SemaphoreType.DMA((particles,)),
            pltpu.SemaphoreType.DMA((6,)),
            pltpu.SemaphoreType.DMA((9,)),
            pltpu.SemaphoreType.DMA((9,)),
        ],
        compiler_params=pltpu.CompilerParams(
            collective_id=0, has_side_effects=True, vmem_limit_bytes=63 * 1024 * 1024
        ),
    )(
        images,
        group_ids,
        row_filters,
        column_filters,
        basis_rows.T,
        basis_columns.T,
        jnp.asarray(soft_edge(pix)),
        rotations,
        references,
        sharpness.reshape(1, particles),
        best_rotation.reshape(1, particles),
        assignments,
    )
    return new_references, evidence.reshape(particles)


def solution(mesh, dims=TORUS):
    in_specs = (
        P(("section", "cls"), None, None),
        P(("section", "cls")),
        P(),
        P(),
        P(),
        P(),
        P("section", None, None),
        P("cls", None),
        P(("section", "cls")),
        P(("section", "cls")),
        P(("section", "cls"), None),
    )
    out_specs = (P("cls", None), P(("section", "cls")))
    return jax.shard_map(
        functools.partial(body, dims), mesh=mesh, in_specs=in_specs, out_specs=out_specs, check_vma=False
    )
```

time: 497 us -> 53.3 us (0.11)
  blocking collectives: 350 us -> 0 us
  starting transfers between devices: 74.3 us -> 0 us
  Pallas kernels: 0 us -> 50 us
  waiting for transfers between devices: 21.3 us -> 0 us
  between operations: 15 us -> 0.64 us
  local copies, waits for them, and re-layouts: 16.5 us -> 2.39 us
  matrix products: 11.8 us -> 0 us
  other arithmetic: 7.26 us -> 0 us
    all_gather x2 -> x0, blocking collectives: 332 us -> none  [the longest x1 320 us: body(): all_refs = lax.all_gather(references, 'cls', axis=0, tiled=True)]
    all_to_all x3 -> x0, starting transfers between devices: 74.3 us -> none  [the longest x1 60.8 us: body(): lax.all_to_all(partial_marg, 'section', split_axis=0, concat_axis=0, tile...]
    pallas_call x0 -> x1, Pallas kernels: none -> 50 us  [body(): pl.pallas_call(functools.partial(kernel, dims), out_shape=(jax.ShapeDtype...]
    all_to_all x3 -> x0, waiting for transfers between devices: 21.2 us -> none  [the longest x1 12.7 us: body(): lax.all_to_all(buffer, 'cls', split_axis=0, concat_axis=0, tiled=True)]
    dot_general x6 -> x0, matrix products: 11.8 us -> none  [the longest x1 5.67 us: filter_images(): jnp.einsum('bij,bjk->bik', row_each, filtered_half, preferred_element_typ...]
    unnamed x2 -> x0, blocking collectives: 9.39 us -> none
    psum x1 -> x0, blocking collectives: 8.29 us -> none  [body(): class_sums, class_weights = lax.psum((class_sums, class_weights), 'section')]
    scatter x2 -> x0, local copies, waits for them, and re-layouts: 6.16 us -> none  [the longest x1 3.78 us: body(): jnp.zeros((classes * capacity,), jnp.bfloat16).at[slot_index]]
  transfers between devices with their start and end apart: 4 -> 0, of which waited for: 2 -> 0; matrix products, arithmetic and copies ran while one was open for 3% -> 0% of each run, Pallas kernels for 0% -> 0%
where the time goes in v1:
time: 53.3 us; the launch traced here: 53 us
  Pallas kernels  50 us (94%)
  local copies, waits for them, and re-layouts  2.39 us (4%)
  between operations  0.64 us (1%)
    pallas_call x1, Pallas kernels, body(): pl.pallas_call(functools.partial(kernel, dims), out_shape=(jax.ShapeDtype...  50 us
    unnamed x2, local copies, waits for them, and re-layouts  2.39 us

profile of v1, /device:TPU:1, one launch (start us, length us, event | category | flops | bytes accessed | tf_op | source)
XLA Modules:
  0.0 53.0 jit_solution(3780911479221170917)
XLA Ops:
  0.6 50.0 %shard_map.131 = (f32[2,256]{1,0:T(2,128)}, f32[1,16]{1,0:T(1,128)}) custom-call(bf16[16,256,256]{2,1,0:T(8,128)(2,1)} %images.1, s32[16]{0:T(128)} %group_ids.1, bf16[4,256,256]{2,1,0:T(8,128)(2,1)} %row_filters.1, bf16[4,256,256]{2,1,0:T(8,128)(2,1)} %column_filters.1, bf16[16,256]{1,0:T(8,128)(2,1)} %bitcast.5, bf16[16,256]{1,0:T(8,128)(2,1)} %bitcast.6, ...), custom_call_target="tpu_custom_call" | custom-call | tf_op jit(solution)/shard_map/pallas_call | solution.py:318
  50.6 1.2 %copy.16 = f32[2,256]{1,0:T(2,128)} copy(f32[2,256]{1,0:T(2,128)} %get-tuple-element.8) | data formatting | bytes 4096
  51.9 1.1 %copy.17 = f32[16]{0:T(128)} copy(f32[16]{0:T(128)} %bitcast.9) | data formatting | bytes 128

commit v2 on v1

--- a/solution.py
+++ b/solution.py
@@ -33,17 +33,17 @@
 def kernel(
     dims,
     images,
-    group_ids,
+    group_ids_hbm,
     row_filters,
     column_filters,
     basis_rows,
     basis_columns,
     mask,
     rotations,
-    references,
-    sharpness,
-    best_rotation,
-    assignments,
+    references_hbm,
+    sharpness_hbm,
+    best_rotation_hbm,
+    assignments_hbm,
     new_references,
     evidence,
     img,
@@ -54,11 +54,17 @@
     bas,
     tiled,
     spread,
+    group_ids,
+    references,
+    sharpness,
+    best_rotation,
+    assignments,
     raw,
     squares,
     near,
     refs,
     coef,
+    turned,
     turned_out,
     turned_in,
     marg_out,
@@ -108,19 +114,26 @@
             (basis_columns, bas.at[1]),
             (mask, edge),
             (rotations, rot),
+            (group_ids_hbm, group_ids),
+            (references_hbm, references),
+            (sharpness_hbm, sharpness),
+            (best_rotation_hbm, best_rotation),
+            (assignments_hbm, assignments),
         ]
     ):
         inputs[k] = pltpu.make_async_copy(src, dst, in_sem.at[k])
-    for k in (2, 3, 0):
+    for k in (2, 3, 6, 0):
         inputs[k].start()
     pltpu.make_async_copy(images.at[0], img.at[0], img_sem.at[0]).start()
-    for k in (1, 4):
+    for k in (1, 4, 7):
         inputs[k].start()
 
     @pl.loop(1, particles)
     def _(n):
         pltpu.make_async_copy(images.at[n], img.at[n], img_sem.at[n]).start()
 
+    for k in (8, 9, 10):
+        inputs[k].start()
     inputs[5].start()
 
     inputs[2].wait()
@@ -134,21 +147,26 @@
     inputs[0].wait()
     inputs[1].wait()
     inputs[4].wait()
-
-    def filter_image(n):
-        pltpu.make_async_copy(images.at[n], img.at[n], img_sem.at[n]).wait()
-        group = group_ids[n]
-        half = jnp.dot(img[n], colf[group], preferred_element_type=jnp.float32).astype(jnp.bfloat16)
-        masked = jnp.dot(rowf[group], half, preferred_element_type=jnp.float32) * edge[...]
-        inner = jnp.dot(masked.astype(jnp.bfloat16), tiled[...], preferred_element_type=jnp.float32)
-        squares[pl.ds(n, 1), :] = jnp.sum(masked * masked, axis=0, keepdims=True)
-        raw[pl.ds(n, 1), :] = jnp.sum(inner * spread[...], axis=0, keepdims=True)
+    inputs[6].wait()
 
     def filter_images(low, high, together):
         @pl.loop(low, high, step=together)
         def _(n):
-            for k in range(together):
-                filter_image(n + k)
+            some = [n + k for k in range(together)]
+            halves = []
+            for m in some:
+                pltpu.make_async_copy(images.at[m], img.at[m], img_sem.at[m]).wait()
+                half = jnp.dot(img[m], colf[group_ids[m]], preferred_element_type=jnp.float32)
+                halves.append(half.astype(jnp.bfloat16))
+            masked = [
+                jnp.dot(rowf[group_ids[m]], half, preferred_element_type=jnp.float32) * edge[...]
+                for m, half in zip(some, halves)
+            ]
+            for m, one in zip(some, masked):
+                squares[pl.ds(m, 1), :] = jnp.sum(one * one, axis=0, keepdims=True)
+            inner = [jnp.dot(one.astype(jnp.bfloat16), tiled[...], preferred_element_type=jnp.float32) for one in masked]
+            for m, one in zip(some, inner):
+                raw[pl.ds(m, 1), :] = jnp.sum(one * spread[...], axis=0, keepdims=True)
 
     def send(k, src, dst, to):
         pltpu.make_async_remote_copy(
@@ -166,27 +184,23 @@
     def sent(k, ref):
         pltpu.make_async_copy(ref, ref, send_sem.at[k]).wait()
 
-    quarter = particles // 4
-    filter_images(0, quarter, 2)
+    filter_images(0, particles // 2, 4)
 
     pl.semaphore_wait(barrier, len(peers))
-    near[0] = references[...].astype(jnp.float32).astype(jnp.bfloat16)
-    for dz in range(1, nz):
-        send(0, near.at[0], near.at[nz - dz], at(dz, 0, 0, 0))
-    filter_images(quarter, 2 * quarter, 2)
-    arrived(0, near.at[pl.ds(1, nz - 1)])
-    refs[0, 0] = jnp.concatenate([near[dz].astype(jnp.float32) for dz in range(nz)], axis=0).astype(jnp.bfloat16)
-    for dy in range(1, ny):
-        send(1, refs.at[0, 0], refs.at[0, ny - dy], at(0, 0, dy, 0))
-    filter_images(2 * quarter, 3 * quarter, 2)
-    arrived(1, refs.at[0, pl.ds(1, ny - 1)])
-    for dx in range(1, nx):
-        send(2, refs.at[0], refs.at[nx - dx], at(0, dx, 0, 0))
-    filter_images(3 * quarter, particles, 2)
+    inputs[7].wait()
+    near[0] = references[...]
+    zl, core = section // 2, section % 2
+    toward = 2 * zl - 1 + nz
+    for dz, low, slot in ((toward, zl, 1 + (nz - 2) * zl), (toward, 1 - zl, 1 + (nz - 2) * zl), (2, 1 - zl, 2)):
+        to = {"section": low * 2 + core, "cls": (((zh + dz) % nz) * nx + xx) * ny + yy}
+        send(0, near.at[0], near.at[slot], to)
+    filter_images(particles // 2, particles, 4)
 
     eye = lax.broadcasted_iota(jnp.int32, (particles, particles), 0) == lax.broadcasted_iota(
         jnp.int32, (particles, particles), 1
     )
+    inputs[8].wait()
+    inputs[9].wait()
     sharp_row = sharpness[...].astype(jnp.float32)
     sharp = jnp.sum(jnp.where(eye, jnp.broadcast_to(sharp_row, (particles, particles)), 0.0), axis=1, keepdims=True)
     best_row = best_rotation[...].astype(jnp.float32)
@@ -198,47 +212,55 @@
     for ds in range(1, sections):
         send(3, coef.at[0], coef.at[sections - ds], at(0, 0, 0, ds))
 
+    arrived(0, near.at[pl.ds(1, nz - 1)])
+    refs[0, 0] = jnp.concatenate([near[dz].astype(jnp.float32) for dz in range(nz)], axis=0).astype(jnp.bfloat16)
+    for dy in range(1, ny):
+        send(1, refs.at[0, 0], refs.at[0, ny - dy], at(0, 0, dy, 0))
+
     place = lax.broadcasted_iota(jnp.int32, (particles, classes), 1)
     dx_at, rest = place // (ny * nz * 2), place % (ny * nz * 2)
     dy_at, rest = rest // (nz * 2), rest % (nz * 2)
     dz_at, last = rest // 2, rest % 2
     name = ((((zh + dz_at) % nz) * nx + (xx + dx_at) % nx) * ny + (yy + dy_at) % ny) * 2 + last
+    inputs[10].wait()
     listed = jnp.zeros((particles, classes), jnp.float32)
     for j in range(assignments.shape[1]):
         listed = jnp.where(assignments[:, j : j + 1] == name, 1.0, listed)
 
     inputs[5].wait()
-    arrived(2, refs.at[pl.ds(1, nx - 1)])
-    all_refs = refs[...].astype(jnp.float32).reshape(classes, width).astype(jnp.bfloat16)
     arrived(3, coef.at[pl.ds(1, sections - 1)])
-
     everyone = sections * particles
     gathered = coef[:, :, 0:width].reshape(everyone, width)
     best_all = coef[:, :, width:].astype(jnp.float32).reshape(everyone, LANES)
     best_all = jnp.concatenate([best_all] * (width // LANES), axis=1)
     first = (section * local).astype(jnp.float32)
     aligned = jnp.zeros((everyone, width), jnp.float32)
-    turned = []
     for r in range(local):
         one = contract_last(gathered, rot[r])
         aligned = jnp.where(best_all == first + float(r), one, aligned)
-        turned.append(one.astype(jnp.bfloat16))
+        turned[pl.ds(r * everyone, everyone), :] = one.astype(jnp.bfloat16)
     turned_out[...] = aligned.astype(jnp.bfloat16).reshape(sections, particles, width)
     for ds in range(1, sections):
         send(4, turned_out.at[ds], turned_in.at[sections - ds], at(0, 0, 0, ds))
-    scores = [contract_last(one, all_refs) for one in turned]
-    largest = functools.reduce(jnp.maximum, scores)
-    total = functools.reduce(jnp.add, [jnp.exp(one - largest) for one in scores])
+
+    arrived(1, refs.at[0, pl.ds(1, ny - 1)])
+    for dx in range(1, nx):
+        send(2, refs.at[0], refs.at[nx - dx], at(0, dx, 0, 0))
+    arrived(4, turned_in.at[pl.ds(1, sections - 1)])
+    mine = functools.reduce(
+        jnp.add, [turned_out[0].astype(jnp.float32)] + [turned_in[d].astype(jnp.float32) for d in range(1, sections)]
+    )
+    mine = (mine * (1.0 / sharp)).astype(jnp.bfloat16)
+    with_one = jnp.concatenate([mine, jnp.ones((particles, LANES), jnp.bfloat16)], axis=1)
+
+    arrived(2, refs.at[pl.ds(1, nx - 1)])
+    all_refs = refs[...].astype(jnp.float32).reshape(classes, width).astype(jnp.bfloat16)
+    scores = contract_last(turned[...], all_refs).reshape(local, everyone, classes)
+    largest = jnp.max(scores, axis=0)
+    total = jnp.sum(jnp.exp(scores - largest), axis=0)
     marg_out[...] = (largest + jnp.log(total)).reshape(sections, particles, classes)
     for ds in range(1, sections):
         send(5, marg_out.at[ds], marg_in.at[sections - ds], at(0, 0, 0, ds))
-
-    arrived(4, turned_in.at[pl.ds(1, sections - 1)])
-    mine = functools.reduce(
-        jnp.add, [turned_out[0].astype(jnp.float32)] + [turned_in[d].astype(jnp.float32) for d in range(1, sections)]
-    )
-    mine = (mine * (1.0 / sharp)).astype(jnp.bfloat16)
-    with_one = jnp.concatenate([mine, jnp.ones((particles, LANES), jnp.bfloat16)], axis=1)
     arrived(5, marg_in.at[pl.ds(1, sections - 1)])
     parts = [marg_out[0]] + [marg_in[d] for d in range(1, sections)]
     largest = functools.reduce(jnp.maximum, parts)
@@ -288,6 +310,17 @@
     sent(6, sum_x.at[pl.ds(1, nx - 1)])
     sent(7, sum_y.at[pl.ds(1, ny - 1)])
     sent(8, got_z.at[pl.ds(0, nz * sections - 1)])
+
+
+def hand_on(sums, proofs, new_references, evidence, sems):
+    copies = [
+        pltpu.make_async_copy(sums, new_references, sems.at[0]),
+        pltpu.make_async_copy(proofs, evidence, sems.at[1]),
+    ]
+    for copy in copies:
+        copy.start()
+    for copy in copies:
+        copy.wait()
 
 
 def body(
@@ -314,14 +347,13 @@
     bf16, f32 = jnp.bfloat16, jnp.float32
     hbm = pl.BlockSpec(memory_space=pltpu.HBM)
     vmem = pl.BlockSpec(memory_space=pltpu.VMEM)
-    smem = pl.BlockSpec(memory_space=pltpu.SMEM)
     new_references, evidence = pl.pallas_call(
         functools.partial(kernel, dims),
         out_shape=(
             jax.ShapeDtypeStruct((2, width), f32),
             jax.ShapeDtypeStruct((1, particles), f32),
         ),
-        in_specs=[hbm, smem, hbm, hbm, hbm, hbm, hbm, hbm, vmem, vmem, vmem, vmem],
+        in_specs=[hbm] * 12,
         out_specs=(vmem, vmem),
         scratch_shapes=[
             pltpu.VMEM((particles, pix, pix), bf16),
@@ -332,11 +364,17 @@
             pltpu.VMEM((2, nb, pix), bf16),
             pltpu.VMEM((pix, nb * nb), bf16),
             pltpu.VMEM((pix, nb * nb), f32),
+            pltpu.SMEM((particles,), jnp.int32),
+            pltpu.VMEM((2, width), bf16),
+            pltpu.VMEM((1, particles), bf16),
+            pltpu.VMEM((1, particles), jnp.int32),
+            pltpu.VMEM(assignments.shape, jnp.int32),
             pltpu.VMEM((particles, nb * nb), f32),
             pltpu.VMEM((particles, pix), f32),
             pltpu.VMEM((nz, 2, width), bf16),
             pltpu.VMEM((nx, ny, 2 * nz, width), bf16),
             pltpu.VMEM((sections, particles, wide), bf16),
+            pltpu.VMEM((local * sections * particles, width), bf16),
             pltpu.VMEM((sections, particles, width), bf16),
             pltpu.VMEM((sections, particles, width), bf16),
             pltpu.VMEM((sections, particles, classes), f32),
@@ -348,7 +386,7 @@
             pltpu.VMEM((nz, 2, wide), f32),
             pltpu.VMEM((nz * sections, 2, wide), f32),
             pltpu.SemaphoreType.DMA((particles,)),
-            pltpu.SemaphoreType.DMA((6,)),
+            pltpu.SemaphoreType.DMA((11,)),
             pltpu.SemaphoreType.DMA((9,)),
             pltpu.SemaphoreType.DMA((9,)),
         ],
@@ -369,6 +407,16 @@
         best_rotation.reshape(1, particles),
         assignments,
     )
+    new_references, evidence = pl.pallas_call(
+        hand_on,
+        out_shape=(
+            jax.ShapeDtypeStruct((2, width), f32),
+            jax.ShapeDtypeStruct((1, particles), f32),
+        ),
+        in_specs=[hbm, hbm],
+        out_specs=(hbm, hbm),
+        scratch_shapes=[pltpu.SemaphoreType.DMA((2,))],
+    )(new_references, evidence)
     return new_references, evidence.reshape(particles)
 
 

time: 53.3 us -> 48.8 us (0.916)
  local copies, waits for them, and re-layouts: 2.39 us -> 0 us
  Pallas kernels: 50 us -> 48 us
    pallas_call x1, Pallas kernels: 50 us -> 46.8 us  [body(): pl.pallas_call(functools.partial(kernel, dims), out_shape=(jax.ShapeDtype...]
    unnamed x2 -> x0, local copies, waits for them, and re-layouts: 2.39 us -> none
    pallas_call x0 -> x1, Pallas kernels: none -> 1.2 us  [body(): pl.pallas_call(hand_on, out_shape=(jax.ShapeDtypeStruct((2, width), f32),...]
where the time goes in v2:
time: 48.8 us; the launch traced here: 48.7 us
  Pallas kernels  48 us (98%)
  between operations  0.64 us (1%)
    pallas_call x1, Pallas kernels, body(): pl.pallas_call(functools.partial(kernel, dims), out_shape=(jax.ShapeDtype...  46.8 us
    pallas_call x1, Pallas kernels, body(): pl.pallas_call(hand_on, out_shape=(jax.ShapeDtypeStruct((2, width), f32),...  1.2 us

profile of v2, /device:TPU:1, one launch (start us, length us, event | category | flops | bytes accessed | tf_op | source)
XLA Modules:
  0.0 48.7 jit_solution(2974569521539902898)
XLA Ops:
  0.6 46.8 %shard_map.131 = (f32[2,256]{1,0:T(2,128)}, f32[1,16]{1,0:T(1,128)}) custom-call(bf16[16,256,256]{2,1,0:T(8,128)(2,1)} %images.1, s32[16]{0:T(128)} %group_ids_hbm.1, bf16[4,256,256]{2,1,0:T(8,128)(2,1)} %row_filters.1, bf16[4,256,256]{2,1,0:T(8,128)(2,1)} %column_filters.1, bf16[16,256]{1,0:T(8,128)(2,1)} %bitcast.5, bf16[16,256]{1,0:T(8,128)(2,1)} %bitcast.6, ...), custom_call_target="tpu_custom_call" | custom-call | tf_op jit(solution)/shard_map/pallas_call | solution.py:350
  47.5 1.2 %shard_map.132 = (f32[2,256]{1,0:T(2,128)}, f32[1,16]{1,0:T(1,128)}) custom-call(f32[2,256]{1,0:T(2,128)} %get-tuple-element.6.sums, f32[1,16]{1,0:T(1,128)} %get-tuple-element.7.proofs), custom_call_target="tpu_custom_call" | custom-call | tf_op jit(solution)/shard_map/pallas_call | solution.py:410

commit v3 on v2

--- a/solution.py
+++ b/solution.py
@@ -69,8 +69,6 @@
     turned_in,
     marg_out,
     marg_in,
-    sum_x,
-    got_x,
     sum_y,
     got_y,
     sum_z,
@@ -269,33 +267,27 @@
     weight = jnp.where(listed > 0.0, jnp.exp(marg - highest), 0.0)
     weight = (weight / jnp.sum(weight, axis=1, keepdims=True)).astype(jnp.bfloat16)
     sums = contract_first(weight, with_one)
-    sum_x[...] = sums.astype(jnp.bfloat16).reshape(sum_x.shape)
-    for dx in range(1, nx):
-        send(6, sum_x.at[dx], got_x.at[dx], at(0, dx, 0, 0))
+    sum_y[...] = sums.reshape(sum_y.shape).astype(jnp.bfloat16)
+    order = [(dx, dy) for dx in range(nx) for dy in range(ny) if (dx, dy) != (0, 0)]
+    for dx, dy in sorted(order, key=lambda d: -min(d[0], nx - d[0]) - min(d[1], ny - d[1])):
+        send(6, sum_y.at[dx * ny + dy], got_y.at[dx * ny + dy], at(0, dx, dy, 0))
 
     peak = jnp.max(marg, axis=1, keepdims=True)
     proof = peak + jnp.log(jnp.sum(jnp.exp(marg - peak), axis=1, keepdims=True))
     evidence[...] = jnp.sum(jnp.where(eye, jnp.broadcast_to(proof, (particles, particles)), 0.0), axis=0, keepdims=True)
 
-    arrived(6, got_x.at[pl.ds(1, nx - 1)])
+    arrived(6, got_y.at[pl.ds(1, nx * ny - 1)])
     total = functools.reduce(
-        jnp.add, [sum_x[0].astype(jnp.float32)] + [got_x[d].astype(jnp.float32) for d in range(1, nx)]
-    )
-    sum_y[...] = total.reshape(sum_y.shape).astype(jnp.bfloat16)
-    for dy in range(1, ny):
-        send(7, sum_y.at[dy], got_y.at[dy], at(0, 0, dy, 0))
-    arrived(7, got_y.at[pl.ds(1, ny - 1)])
-    total = functools.reduce(
-        jnp.add, [sum_y[0].astype(jnp.float32)] + [got_y[d].astype(jnp.float32) for d in range(1, ny)]
+        jnp.add, [sum_y[0].astype(jnp.float32)] + [got_y[d].astype(jnp.float32) for d in range(1, nx * ny)]
     )
     for dz in range(nz):
         sum_z[dz] = total[2 * dz : 2 * dz + 2]
     for dz in range(nz):
         for ds in range(sections):
             if (dz, ds) != (0, 0):
-                send(8, sum_z.at[dz], got_z.at[dz * sections + section], at(dz, 0, 0, ds))
+                send(7, sum_z.at[dz], got_z.at[dz * sections + section], at(dz, 0, 0, ds))
     got_z[section] = sum_z[0]
-    arrived(8, got_z.at[pl.ds(0, nz * sections - 1)])
+    arrived(7, got_z.at[pl.ds(0, nz * sections - 1)])
     total = functools.reduce(jnp.add, [got_z[d] for d in range(nz * sections)])
     over = total[:, width:] + 1.0
     over = jnp.concatenate([over] * (width // LANES), axis=1)
@@ -307,9 +299,8 @@
     sent(3, coef.at[pl.ds(1, sections - 1)])
     sent(4, turned_out.at[pl.ds(1, sections - 1)])
     sent(5, marg_out.at[pl.ds(1, sections - 1)])
-    sent(6, sum_x.at[pl.ds(1, nx - 1)])
-    sent(7, sum_y.at[pl.ds(1, ny - 1)])
-    sent(8, got_z.at[pl.ds(0, nz * sections - 1)])
+    sent(6, sum_y.at[pl.ds(1, nx * ny - 1)])
+    sent(7, got_z.at[pl.ds(0, nz * sections - 1)])
 
 
 def hand_on(sums, proofs, new_references, evidence, sems):
@@ -379,16 +370,14 @@
             pltpu.VMEM((sections, particles, width), bf16),
             pltpu.VMEM((sections, particles, classes), f32),
             pltpu.VMEM((sections, particles, classes), f32),
-            pltpu.VMEM((nx, 2 * ny * nz, wide), bf16),
-            pltpu.VMEM((nx, 2 * ny * nz, wide), bf16),
-            pltpu.VMEM((ny, 2 * nz, wide), bf16),
-            pltpu.VMEM((ny, 2 * nz, wide), bf16),
+            pltpu.VMEM((nx * ny, 2 * nz, wide), bf16),
+            pltpu.VMEM((nx * ny, 2 * nz, wide), bf16),
             pltpu.VMEM((nz, 2, wide), f32),
             pltpu.VMEM((nz * sections, 2, wide), f32),
             pltpu.SemaphoreType.DMA((particles,)),
             pltpu.SemaphoreType.DMA((11,)),
-            pltpu.SemaphoreType.DMA((9,)),
-            pltpu.SemaphoreType.DMA((9,)),
+            pltpu.SemaphoreType.DMA((8,)),
+            pltpu.SemaphoreType.DMA((8,)),
         ],
         compiler_params=pltpu.CompilerParams(
             collective_id=0, has_side_effects=True, vmem_limit_bytes=63 * 1024 * 1024

time: 48.8 us -> 46.6 us (0.955)
  Pallas kernels: 48 us -> 45.8 us
    pallas_call x1, Pallas kernels: 46.8 us -> 44.6 us  [body(): pl.pallas_call(functools.partial(kernel, dims), out_shape=(jax.ShapeDtype...]
where the time goes in v3:
time: 46.6 us; the launch traced here: 46.4 us
  Pallas kernels  45.8 us (98%)
  between operations  0.64 us (1%)
    pallas_call x1, Pallas kernels, body(): pl.pallas_call(functools.partial(kernel, dims), out_shape=(jax.ShapeDtype...  44.6 us
    pallas_call x1, Pallas kernels, body(): pl.pallas_call(hand_on, out_shape=(jax.ShapeDtypeStruct((2, width), f32),...  1.2 us

profile of v3, /device:TPU:1, one launch (start us, length us, event | category | flops | bytes accessed | tf_op | source)
XLA Modules:
  0.0 46.4 jit_solution(18352511503272937761)
XLA Ops:
  0.6 44.6 %shard_map.131 = (f32[2,256]{1,0:T(2,128)}, f32[1,16]{1,0:T(1,128)}) custom-call(bf16[16,256,256]{2,1,0:T(8,128)(2,1)} %images.1, s32[16]{0:T(128)} %group_ids_hbm.1, bf16[4,256,256]{2,1,0:T(8,128)(2,1)} %row_filters.1, bf16[4,256,256]{2,1,0:T(8,128)(2,1)} %column_filters.1, bf16[16,256]{1,0:T(8,128)(2,1)} %bitcast.5, bf16[16,256]{1,0:T(8,128)(2,1)} %bitcast.6, ...), custom_call_target="tpu_custom_call" | custom-call | tf_op jit(solution)/shard_map/pallas_call | solution.py:341
  45.2 1.2 %shard_map.132 = (f32[2,256]{1,0:T(2,128)}, f32[1,16]{1,0:T(1,128)}) custom-call(f32[2,256]{1,0:T(2,128)} %get-tuple-element.6.sums, f32[1,16]{1,0:T(1,128)} %get-tuple-element.7.proofs), custom_call_target="tpu_custom_call" | custom-call | tf_op jit(solution)/shard_map/pallas_call | solution.py:399

commit v4 on v3

--- a/solution.py
+++ b/solution.py
@@ -63,6 +63,7 @@
     squares,
     near,
     refs,
+    reorder,
     coef,
     turned,
     turned_out,
@@ -77,6 +78,7 @@
     in_sem,
     send_sem,
     recv_sem,
+    ready,
 ):
     nz, nx, ny = dims
     section, cls = lax.axis_index("section"), lax.axis_index("cls")
@@ -96,9 +98,15 @@
             "cls": (((zh + dz) % nz) * nx + (xx + dx) % nx) * ny + (yy + dy) % ny,
         }
 
+    zl, core = section // 2, section % 2
+
+    def above(dz, low):
+        return {"section": low * 2 + core, "cls": (((zh + dz) % nz) * nx + xx) * ny + yy}
+
     peers = [at(0, dx, 0, 0) for dx in range(1, nx)]
     peers += [at(0, 0, dy, 0) for dy in range(1, ny)]
-    peers += [at(dz, 0, 0, ds) for dz in range(nz) for ds in range(sections) if (dz, ds) != (0, 0)]
+    peers += [at(0, 0, 0, ds) for ds in range(1, sections)]
+    peers += [above(1, 0), above(nz - 1, 1), above(2, 1 - zl)]
     barrier = pltpu.get_barrier_semaphore()
     for peer in peers:
         pl.semaphore_signal(barrier, inc=1, device_id=peer, device_id_type=MESH)
@@ -187,11 +195,10 @@
     pl.semaphore_wait(barrier, len(peers))
     inputs[7].wait()
     near[0] = references[...]
-    zl, core = section // 2, section % 2
-    toward = 2 * zl - 1 + nz
-    for dz, low, slot in ((toward, zl, 1 + (nz - 2) * zl), (toward, 1 - zl, 1 + (nz - 2) * zl), (2, 1 - zl, 2)):
-        to = {"section": low * 2 + core, "cls": (((zh + dz) % nz) * nx + xx) * ny + yy}
-        send(0, near.at[0], near.at[slot], to)
+    for dy in range(1, ny):
+        send(0, near.at[0], near.at[ny - dy], at(0, 0, dy, 0))
+    for dx in range(1, nx):
+        pl.semaphore_signal(ready, inc=1, device_id=at(0, dx, 0, 0), device_id_type=MESH)
     filter_images(particles // 2, particles, 4)
 
     eye = lax.broadcasted_iota(jnp.int32, (particles, particles), 0) == lax.broadcasted_iota(
@@ -208,25 +215,39 @@
     coef[0, :, 0:width] = (raw[...] * scale).astype(jnp.bfloat16)
     coef[0, :, width:] = jnp.broadcast_to(best, (particles, LANES)).astype(jnp.bfloat16)
     for ds in range(1, sections):
-        send(3, coef.at[0], coef.at[sections - ds], at(0, 0, 0, ds))
-
-    arrived(0, near.at[pl.ds(1, nz - 1)])
-    refs[0, 0] = jnp.concatenate([near[dz].astype(jnp.float32) for dz in range(nz)], axis=0).astype(jnp.bfloat16)
-    for dy in range(1, ny):
-        send(1, refs.at[0, 0], refs.at[0, ny - dy], at(0, 0, dy, 0))
+        send(2, coef.at[0], coef.at[sections - ds], at(0, 0, 0, ds))
+
+    arrived(0, near.at[pl.ds(1, ny - 1)])
+    refs[0] = jnp.concatenate([near[dy].astype(jnp.float32) for dy in range(ny)], axis=0).astype(jnp.bfloat16)
+    pl.semaphore_wait(ready, nx - 1)
+    side = 1 + (nz - 2) * zl
+    for dx in (2, 1, 3, 0):
+        if dx >= nx:
+            continue
+        for dz, low, slot in ((2, 1 - zl, 2), (2 * zl - 1 + nz, zl, side), (2 * zl - 1 + nz, 1 - zl, side), (0, zl, 0)):
+            if dx or not isinstance(dz, int) or dz:
+                to = {"section": low * 2 + core, "cls": (((zh + dz) % nz) * nx + (xx + dx) % nx) * ny + yy}
+                send(1, refs.at[0], refs.at[(nx - dx) % nx * nz + slot], to)
 
     place = lax.broadcasted_iota(jnp.int32, (particles, classes), 1)
-    dx_at, rest = place // (ny * nz * 2), place % (ny * nz * 2)
-    dy_at, rest = rest // (nz * 2), rest % (nz * 2)
-    dz_at, last = rest // 2, rest % 2
+    dx_at, rest = place // (nz * ny * 2), place % (nz * ny * 2)
+    dz_at, rest = rest // (ny * 2), rest % (ny * 2)
+    dy_at, last = rest // 2, rest % 2
     name = ((((zh + dz_at) % nz) * nx + (xx + dx_at) % nx) * ny + (yy + dy_at) % ny) * 2 + last
     inputs[10].wait()
     listed = jnp.zeros((particles, classes), jnp.float32)
     for j in range(assignments.shape[1]):
         listed = jnp.where(assignments[:, j : j + 1] == name, 1.0, listed)
 
+    place = lax.broadcasted_iota(jnp.int32, (classes, classes), 1)
+    dx_at, rest = place // (ny * nz * 2), place % (ny * nz * 2)
+    dy_at, rest = rest // (nz * 2), rest % (nz * 2)
+    place = dx_at * (nz * ny * 2) + (rest // 2) * (ny * 2) + dy_at * 2 + rest % 2
+    place = place == lax.broadcasted_iota(jnp.int32, (classes, classes), 0)
+    reorder[...] = jnp.where(place, 1.0, 0.0).astype(jnp.bfloat16)
+
     inputs[5].wait()
-    arrived(3, coef.at[pl.ds(1, sections - 1)])
+    arrived(2, coef.at[pl.ds(1, sections - 1)])
     everyone = sections * particles
     gathered = coef[:, :, 0:width].reshape(everyone, width)
     best_all = coef[:, :, width:].astype(jnp.float32).reshape(everyone, LANES)
@@ -239,44 +260,42 @@
         turned[pl.ds(r * everyone, everyone), :] = one.astype(jnp.bfloat16)
     turned_out[...] = aligned.astype(jnp.bfloat16).reshape(sections, particles, width)
     for ds in range(1, sections):
-        send(4, turned_out.at[ds], turned_in.at[sections - ds], at(0, 0, 0, ds))
-
-    arrived(1, refs.at[0, pl.ds(1, ny - 1)])
-    for dx in range(1, nx):
-        send(2, refs.at[0], refs.at[nx - dx], at(0, dx, 0, 0))
-    arrived(4, turned_in.at[pl.ds(1, sections - 1)])
+        send(3, turned_out.at[ds], turned_in.at[sections - ds], at(0, 0, 0, ds))
+
+    arrived(3, turned_in.at[pl.ds(1, sections - 1)])
     mine = functools.reduce(
         jnp.add, [turned_out[0].astype(jnp.float32)] + [turned_in[d].astype(jnp.float32) for d in range(1, sections)]
     )
     mine = (mine * (1.0 / sharp)).astype(jnp.bfloat16)
     with_one = jnp.concatenate([mine, jnp.ones((particles, LANES), jnp.bfloat16)], axis=1)
 
-    arrived(2, refs.at[pl.ds(1, nx - 1)])
-    all_refs = refs[...].astype(jnp.float32).reshape(classes, width).astype(jnp.bfloat16)
+    arrived(1, refs.at[pl.ds(1, nx * nz - 1)])
+    all_refs = refs[...].reshape(classes, width)
     scores = contract_last(turned[...], all_refs).reshape(local, everyone, classes)
     largest = jnp.max(scores, axis=0)
     total = jnp.sum(jnp.exp(scores - largest), axis=0)
     marg_out[...] = (largest + jnp.log(total)).reshape(sections, particles, classes)
     for ds in range(1, sections):
-        send(5, marg_out.at[ds], marg_in.at[sections - ds], at(0, 0, 0, ds))
-    arrived(5, marg_in.at[pl.ds(1, sections - 1)])
+        send(4, marg_out.at[ds], marg_in.at[sections - ds], at(0, 0, 0, ds))
+    arrived(4, marg_in.at[pl.ds(1, sections - 1)])
     parts = [marg_out[0]] + [marg_in[d] for d in range(1, sections)]
     largest = functools.reduce(jnp.maximum, parts)
     marg = largest + jnp.log(functools.reduce(jnp.add, [jnp.exp(one - largest) for one in parts]))
     highest = jnp.max(jnp.where(listed > 0.0, marg, -jnp.inf), axis=1, keepdims=True)
     weight = jnp.where(listed > 0.0, jnp.exp(marg - highest), 0.0)
     weight = (weight / jnp.sum(weight, axis=1, keepdims=True)).astype(jnp.bfloat16)
+    weight = jnp.dot(weight, reorder[...], preferred_element_type=jnp.float32).astype(jnp.bfloat16)
     sums = contract_first(weight, with_one)
     sum_y[...] = sums.reshape(sum_y.shape).astype(jnp.bfloat16)
     order = [(dx, dy) for dx in range(nx) for dy in range(ny) if (dx, dy) != (0, 0)]
     for dx, dy in sorted(order, key=lambda d: -min(d[0], nx - d[0]) - min(d[1], ny - d[1])):
-        send(6, sum_y.at[dx * ny + dy], got_y.at[dx * ny + dy], at(0, dx, dy, 0))
+        send(5, sum_y.at[dx * ny + dy], got_y.at[dx * ny + dy], at(0, dx, dy, 0))
 
     peak = jnp.max(marg, axis=1, keepdims=True)
     proof = peak + jnp.log(jnp.sum(jnp.exp(marg - peak), axis=1, keepdims=True))
     evidence[...] = jnp.sum(jnp.where(eye, jnp.broadcast_to(proof, (particles, particles)), 0.0), axis=0, keepdims=True)
 
-    arrived(6, got_y.at[pl.ds(1, nx * ny - 1)])
+    arrived(5, got_y.at[pl.ds(1, nx * ny - 1)])
     total = functools.reduce(
         jnp.add, [sum_y[0].astype(jnp.float32)] + [got_y[d].astype(jnp.float32) for d in range(1, nx * ny)]
     )
@@ -285,22 +304,21 @@
     for dz in range(nz):
         for ds in range(sections):
             if (dz, ds) != (0, 0):
-                send(7, sum_z.at[dz], got_z.at[dz * sections + section], at(dz, 0, 0, ds))
+                send(6, sum_z.at[dz], got_z.at[dz * sections + section], at(dz, 0, 0, ds))
     got_z[section] = sum_z[0]
-    arrived(7, got_z.at[pl.ds(0, nz * sections - 1)])
+    arrived(6, got_z.at[pl.ds(0, nz * sections - 1)])
     total = functools.reduce(jnp.add, [got_z[d] for d in range(nz * sections)])
     over = total[:, width:] + 1.0
     over = jnp.concatenate([over] * (width // LANES), axis=1)
     new_references[...] = (total[:, 0:width] + references[...].astype(jnp.float32)) / over
 
-    sent(0, near.at[pl.ds(1, nz - 1)])
-    sent(1, refs.at[0, pl.ds(1, ny - 1)])
-    sent(2, refs.at[pl.ds(1, nx - 1)])
-    sent(3, coef.at[pl.ds(1, sections - 1)])
-    sent(4, turned_out.at[pl.ds(1, sections - 1)])
-    sent(5, marg_out.at[pl.ds(1, sections - 1)])
-    sent(6, sum_y.at[pl.ds(1, nx * ny - 1)])
-    sent(7, got_z.at[pl.ds(0, nz * sections - 1)])
+    sent(0, near.at[pl.ds(1, ny - 1)])
+    sent(1, refs.at[pl.ds(1, nx * nz - 1)])
+    sent(2, coef.at[pl.ds(1, sections - 1)])
+    sent(3, turned_out.at[pl.ds(1, sections - 1)])
+    sent(4, marg_out.at[pl.ds(1, sections - 1)])
+    sent(5, sum_y.at[pl.ds(1, nx * ny - 1)])
+    sent(6, got_z.at[pl.ds(0, nz * sections - 1)])
 
 
 def hand_on(sums, proofs, new_references, evidence, sems):
@@ -362,8 +380,9 @@
             pltpu.VMEM(assignments.shape, jnp.int32),
             pltpu.VMEM((particles, nb * nb), f32),
             pltpu.VMEM((particles, pix), f32),
-            pltpu.VMEM((nz, 2, width), bf16),
-            pltpu.VMEM((nx, ny, 2 * nz, width), bf16),
+            pltpu.VMEM((ny, 2, width), bf16),
+            pltpu.VMEM((nx * nz, 2 * ny, width), bf16),
+            pltpu.VMEM((classes, classes), bf16),
             pltpu.VMEM((sections, particles, wide), bf16),
             pltpu.VMEM((local * sections * particles, width), bf16),
             pltpu.VMEM((sections, particles, width), bf16),
@@ -376,8 +395,9 @@
             pltpu.VMEM((nz * sections, 2, wide), f32),
             pltpu.SemaphoreType.DMA((particles,)),
             pltpu.SemaphoreType.DMA((11,)),
-            pltpu.SemaphoreType.DMA((8,)),
-            pltpu.SemaphoreType.DMA((8,)),
+            pltpu.SemaphoreType.DMA((7,)),
+            pltpu.SemaphoreType.DMA((7,)),
+            pltpu.SemaphoreType.REGULAR,
         ],
         compiler_params=pltpu.CompilerParams(
             collective_id=0, has_side_effects=True, vmem_limit_bytes=63 * 1024 * 1024

time: 46.6 us -> 44.4 us (0.953)
  Pallas kernels: 45.8 us -> 43.6 us
    pallas_call x1, Pallas kernels: 44.6 us -> 42.4 us  [body(): pl.pallas_call(functools.partial(kernel, dims), out_shape=(jax.ShapeDtype...]
where the time goes in v4:
time: 44.4 us; the launch traced here: 44.3 us
  Pallas kernels  43.6 us (98%)
  between operations  0.64 us (1%)
    pallas_call x1, Pallas kernels, body(): pl.pallas_call(functools.partial(kernel, dims), out_shape=(jax.ShapeDtype...  42.4 us
    pallas_call x1, Pallas kernels, body(): pl.pallas_call(hand_on, out_shape=(jax.ShapeDtypeStruct((2, width), f32),...  1.2 us

profile of v4, /device:TPU:1, one launch (start us, length us, event | category | flops | bytes accessed | tf_op | source)
XLA Modules:
  0.0 44.3 jit_solution(1191394042651473888)
XLA Ops:
  0.6 42.4 %shard_map.131 = (f32[2,256]{1,0:T(2,128)}, f32[1,16]{1,0:T(1,128)}) custom-call(bf16[16,256,256]{2,1,0:T(8,128)(2,1)} %images.1, s32[16]{0:T(128)} %group_ids_hbm.1, bf16[4,256,256]{2,1,0:T(8,128)(2,1)} %row_filters.1, bf16[4,256,256]{2,1,0:T(8,128)(2,1)} %column_filters.1, bf16[16,256]{1,0:T(8,128)(2,1)} %bitcast.5, bf16[16,256]{1,0:T(8,128)(2,1)} %bitcast.6, ...), custom_call_target="tpu_custom_call" | custom-call | tf_op jit(solution)/shard_map/pallas_call | solution.py:359
  43.1 1.2 %shard_map.132 = (f32[2,256]{1,0:T(2,128)}, f32[1,16]{1,0:T(1,128)}) custom-call(f32[2,256]{1,0:T(2,128)} %get-tuple-element.6.sums, f32[1,16]{1,0:T(1,128)} %get-tuple-element.7.proofs), custom_call_target="tpu_custom_call" | custom-call | tf_op jit(solution)/shard_map/pallas_call | solution.py:419

commit v5 on v4

--- a/solution.py
+++ b/solution.py
@@ -359,8 +359,8 @@
     new_references, evidence = pl.pallas_call(
         functools.partial(kernel, dims),
         out_shape=(
-            jax.ShapeDtypeStruct((2, width), f32),
-            jax.ShapeDtypeStruct((1, particles), f32),
+            pltpu.VMEM((2, width), f32),
+            pltpu.VMEM((1, particles), f32),
         ),
         in_specs=[hbm] * 12,
         out_specs=(vmem, vmem),
@@ -422,9 +422,10 @@
             jax.ShapeDtypeStruct((2, width), f32),
             jax.ShapeDtypeStruct((1, particles), f32),
         ),
-        in_specs=[hbm, hbm],
+        in_specs=[vmem, vmem],
         out_specs=(hbm, hbm),
         scratch_shapes=[pltpu.SemaphoreType.DMA((2,))],
+        compiler_params=pltpu.CompilerParams(vmem_limit_bytes=1024 * 1024),
     )(new_references, evidence)
     return new_references, evidence.reshape(particles)
 

time: 44.4 us -> 43.2 us (0.973)
  Pallas kernels: 43.6 us -> 42.5 us
    pallas_call x1, Pallas kernels: 1.2 us -> 0.6 us  [body(): pl.pallas_call(hand_on, out_shape=(jax.ShapeDtypeStruct((2, width), f32),...]
    pallas_call x1, Pallas kernels: 42.4 us -> 41.9 us  [body(): pl.pallas_call(functools.partial(kernel, dims), out_shape=(pltpu.VMEM((2,...]
where the time goes in v5:
time: 43.2 us; the launch traced here: 43.1 us
  Pallas kernels  42.5 us (98%)
  between operations  0.64 us (1%)
    pallas_call x1, Pallas kernels, body(): pl.pallas_call(functools.partial(kernel, dims), out_shape=(pltpu.VMEM((2,...  41.9 us

profile of v5, /device:TPU:1, one launch (start us, length us, event | category | flops | bytes accessed | tf_op | source)
XLA Modules:
  0.0 43.1 jit_solution(4744851128402634165)
XLA Ops:
  0.6 41.9 %shard_map.131 = (f32[2,256]{1,0:T(2,128)S(1)}, f32[1,16]{1,0:T(1,128)S(1)}) custom-call(bf16[16,256,256]{2,1,0:T(8,128)(2,1)} %images.1, s32[16]{0:T(128)} %group_ids_hbm.1, bf16[4,256,256]{2,1,0:T(8,128)(2,1)} %row_filters.1, bf16[4,256,256]{2,1,0:T(8,128)(2,1)} %column_filters.1, bf16[16,256]{1,0:T(8,128)(2,1)} %bitcast.5, bf16[16,256]{1,0:T(8,128)(2,1)} %bitcast.6, ...), custom_call_target="tpu_custom_call" | custom-call | tf_op jit(solution)/shard_map/pallas_call | solution.py:359
  42.5 0.6 %shard_map.132 = (f32[2,256]{1,0:T(2,128)}, f32[1,16]{1,0:T(1,128)}) custom-call(f32[2,256]{1,0:T(2,128)S(1)} %get-tuple-element.6.sums, f32[1,16]{1,0:T(1,128)S(1)} %get-tuple-element.7.proofs), custom_call_target="tpu_custom_call" | custom-call | tf_op jit(solution)/shard_map/pallas_call | solution.py:419

commit v6 on v5

--- a/solution.py
+++ b/solution.py
@@ -103,10 +103,14 @@
     def above(dz, low):
         return {"section": low * 2 + core, "cls": (((zh + dz) % nz) * nx + xx) * ny + yy}
 
-    peers = [at(0, dx, 0, 0) for dx in range(1, nx)]
-    peers += [at(0, 0, dy, 0) for dy in range(1, ny)]
-    peers += [at(0, 0, 0, ds) for ds in range(1, sections)]
-    peers += [above(1, 0), above(nz - 1, 1), above(2, 1 - zl)]
+    along_y = sorted(range(1, ny), key=lambda d: -min(d, ny - d))
+    along_x = sorted(range(1, nx), key=lambda d: -min(d, nx - d))
+    along_z = sorted(range(nz), key=lambda d: -min(d, nz - d))
+    inside = (2, 1, 3)
+    peers = [at(0, 0, dy, 0) for dy in along_y]
+    peers += [above(2, 1 - zl), above(1, 0), above(nz - 1, 1)]
+    peers += [at(0, dx, 0, 0) for dx in along_x]
+    peers += [at(0, 0, 0, ds) for ds in inside]
     barrier = pltpu.get_barrier_semaphore()
     for peer in peers:
         pl.semaphore_signal(barrier, inc=1, device_id=peer, device_id_type=MESH)
@@ -190,16 +194,16 @@
     def sent(k, ref):
         pltpu.make_async_copy(ref, ref, send_sem.at[k]).wait()
 
-    filter_images(0, particles // 2, 4)
+    filter_images(0, particles // 4, 4)
 
     pl.semaphore_wait(barrier, len(peers))
     inputs[7].wait()
     near[0] = references[...]
-    for dy in range(1, ny):
+    for dy in along_y:
         send(0, near.at[0], near.at[ny - dy], at(0, 0, dy, 0))
-    for dx in range(1, nx):
+    for dx in along_x:
         pl.semaphore_signal(ready, inc=1, device_id=at(0, dx, 0, 0), device_id_type=MESH)
-    filter_images(particles // 2, particles, 4)
+    filter_images(particles // 4, particles, 4)
 
     eye = lax.broadcasted_iota(jnp.int32, (particles, particles), 0) == lax.broadcasted_iota(
         jnp.int32, (particles, particles), 1
@@ -214,7 +218,7 @@
     scale = lax.rsqrt(power + EPSILON) * sharp
     coef[0, :, 0:width] = (raw[...] * scale).astype(jnp.bfloat16)
     coef[0, :, width:] = jnp.broadcast_to(best, (particles, LANES)).astype(jnp.bfloat16)
-    for ds in range(1, sections):
+    for ds in inside:
         send(2, coef.at[0], coef.at[sections - ds], at(0, 0, 0, ds))
 
     arrived(0, near.at[pl.ds(1, ny - 1)])
@@ -259,7 +263,7 @@
         aligned = jnp.where(best_all == first + float(r), one, aligned)
         turned[pl.ds(r * everyone, everyone), :] = one.astype(jnp.bfloat16)
     turned_out[...] = aligned.astype(jnp.bfloat16).reshape(sections, particles, width)
-    for ds in range(1, sections):
+    for ds in inside:
         send(3, turned_out.at[ds], turned_in.at[sections - ds], at(0, 0, 0, ds))
 
     arrived(3, turned_in.at[pl.ds(1, sections - 1)])
@@ -275,7 +279,7 @@
     largest = jnp.max(scores, axis=0)
     total = jnp.sum(jnp.exp(scores - largest), axis=0)
     marg_out[...] = (largest + jnp.log(total)).reshape(sections, particles, classes)
-    for ds in range(1, sections):
+    for ds in inside:
         send(4, marg_out.at[ds], marg_in.at[sections - ds], at(0, 0, 0, ds))
     arrived(4, marg_in.at[pl.ds(1, sections - 1)])
     parts = [marg_out[0]] + [marg_in[d] for d in range(1, sections)]
@@ -301,8 +305,8 @@
     )
     for dz in range(nz):
         sum_z[dz] = total[2 * dz : 2 * dz + 2]
-    for dz in range(nz):
-        for ds in range(sections):
+    for dz in along_z:
+        for ds in (*inside, 0):
             if (dz, ds) != (0, 0):
                 send(6, sum_z.at[dz], got_z.at[dz * sections + section], at(dz, 0, 0, ds))
     got_z[section] = sum_z[0]

time: 43.2 us -> 42.4 us (0.981)
  Pallas kernels: 42.5 us -> 41.6 us
    pallas_call x1, Pallas kernels: 41.9 us -> 41 us  [body(): pl.pallas_call(functools.partial(kernel, dims), out_shape=(pltpu.VMEM((2,...]
where the time goes in v6:
time: 42.4 us; the launch traced here: 42.2 us
  Pallas kernels  41.6 us (98%)
  between operations  0.64 us (2%)
    pallas_call x1, Pallas kernels, body(): pl.pallas_call(functools.partial(kernel, dims), out_shape=(pltpu.VMEM((2,...  41 us

profile of v6, /device:TPU:1, one launch (start us, length us, event | category | flops | bytes accessed | tf_op | source)
XLA Modules:
  0.0 42.2 jit_solution(2687364067110101066)
XLA Ops:
  0.6 41.0 %shard_map.131 = (f32[2,256]{1,0:T(2,128)S(1)}, f32[1,16]{1,0:T(1,128)S(1)}) custom-call(bf16[16,256,256]{2,1,0:T(8,128)(2,1)} %images.1, s32[16]{0:T(128)} %group_ids_hbm.1, bf16[4,256,256]{2,1,0:T(8,128)(2,1)} %row_filters.1, bf16[4,256,256]{2,1,0:T(8,128)(2,1)} %column_filters.1, bf16[16,256]{1,0:T(8,128)(2,1)} %bitcast.5, bf16[16,256]{1,0:T(8,128)(2,1)} %bitcast.6, ...), custom_call_target="tpu_custom_call" | custom-call | tf_op jit(solution)/shard_map/pallas_call | solution.py:363
  41.6 0.6 %shard_map.132 = (f32[2,256]{1,0:T(2,128)}, f32[1,16]{1,0:T(1,128)}) custom-call(f32[2,256]{1,0:T(2,128)S(1)} %get-tuple-element.6.sums, f32[1,16]{1,0:T(1,128)S(1)} %get-tuple-element.7.proofs), custom_call_target="tpu_custom_call" | custom-call | tf_op jit(solution)/shard_map/pallas_call | solution.py:423

commit v7 on v6

--- a/solution.py
+++ b/solution.py
@@ -203,7 +203,7 @@
         send(0, near.at[0], near.at[ny - dy], at(0, 0, dy, 0))
     for dx in along_x:
         pl.semaphore_signal(ready, inc=1, device_id=at(0, dx, 0, 0), device_id_type=MESH)
-    filter_images(particles // 4, particles, 4)
+    filter_images(particles // 4, particles, 6)
 
     eye = lax.broadcasted_iota(jnp.int32, (particles, particles), 0) == lax.broadcasted_iota(
         jnp.int32, (particles, particles), 1
@@ -281,6 +281,9 @@
     marg_out[...] = (largest + jnp.log(total)).reshape(sections, particles, classes)
     for ds in inside:
         send(4, marg_out.at[ds], marg_in.at[sections - ds], at(0, 0, 0, ds))
+    order = [(dx, dy) for dx in range(nx) for dy in range(ny) if (dx, dy) != (0, 0)]
+    order = sorted(order, key=lambda d: -min(d[0], nx - d[0]) - min(d[1], ny - d[1]))
+    owners = [at(0, dx, dy, 0) for dx, dy in order]
     arrived(4, marg_in.at[pl.ds(1, sections - 1)])
     parts = [marg_out[0]] + [marg_in[d] for d in range(1, sections)]
     largest = functools.reduce(jnp.maximum, parts)
@@ -291,9 +294,8 @@
     weight = jnp.dot(weight, reorder[...], preferred_element_type=jnp.float32).astype(jnp.bfloat16)
     sums = contract_first(weight, with_one)
     sum_y[...] = sums.reshape(sum_y.shape).astype(jnp.bfloat16)
-    order = [(dx, dy) for dx in range(nx) for dy in range(ny) if (dx, dy) != (0, 0)]
-    for dx, dy in sorted(order, key=lambda d: -min(d[0], nx - d[0]) - min(d[1], ny - d[1])):
-        send(5, sum_y.at[dx * ny + dy], got_y.at[dx * ny + dy], at(0, dx, dy, 0))
+    for (dx, dy), owner in zip(order, owners):
+        send(5, sum_y.at[dx * ny + dy], got_y.at[dx * ny + dy], owner)
 
     peak = jnp.max(marg, axis=1, keepdims=True)
     proof = peak + jnp.log(jnp.sum(jnp.exp(marg - peak), axis=1, keepdims=True))

time: 42.4 us -> 42.2 us (level)
  no operation moved by 1% of the time
where the time goes in v7:
time: 42.2 us; the launch traced here: 42.1 us
  Pallas kernels  41.4 us (98%)
  between operations  0.64 us (2%)
    pallas_call x1, Pallas kernels, body(): pl.pallas_call(functools.partial(kernel, dims), out_shape=(pltpu.VMEM((2,...  40.8 us

profile of v7, /device:TPU:1, one launch (start us, length us, event | category | flops | bytes accessed | tf_op | source)
XLA Modules:
  0.0 42.1 jit_solution(5752501690476781052)
XLA Ops:
  0.6 40.8 %shard_map.131 = (f32[2,256]{1,0:T(2,128)S(1)}, f32[1,16]{1,0:T(1,128)S(1)}) custom-call(bf16[16,256,256]{2,1,0:T(8,128)(2,1)} %images.1, s32[16]{0:T(128)} %group_ids_hbm.1, bf16[4,256,256]{2,1,0:T(8,128)(2,1)} %row_filters.1, bf16[4,256,256]{2,1,0:T(8,128)(2,1)} %column_filters.1, bf16[16,256]{1,0:T(8,128)(2,1)} %bitcast.5, bf16[16,256]{1,0:T(8,128)(2,1)} %bitcast.6, ...), custom_call_target="tpu_custom_call" | custom-call | tf_op jit(solution)/shard_map/pallas_call | solution.py:365
  41.5 0.6 %shard_map.132 = (f32[2,256]{1,0:T(2,128)}, f32[1,16]{1,0:T(1,128)}) custom-call(f32[2,256]{1,0:T(2,128)S(1)} %get-tuple-element.6.sums, f32[1,16]{1,0:T(1,128)S(1)} %get-tuple-element.7.proofs), custom_call_target="tpu_custom_call" | custom-call | tf_op jit(solution)/shard_map/pallas_call | solution.py:425
